TPU v7x, 32 devices: a whole 2x2x4 slice. The times are simulated.
32 devices in a mesh: row: 2 (over y), col: 16 (over z, x, core).
Axes of the slice: x: 2, y: 2, z: 4, core: 2. Of those that a mesh axis runs over, the one named last changes fastest.
Arguments:
- tokens: bfloat16 [25088, 1024], P(('col', 'row')), may hold values from -6 to 6
- w_qkv: bfloat16 [1024, 3072], P('row', 'col'), may hold values from -0.1875 to 0.1875
- w_proj: bfloat16 [1024, 1024], P('row', 'col'), may hold values from -6 to 6
- w_fc1: bfloat16 [1024, 4096], P('row', 'col'), may hold values from -0.1875 to 0.1875
- w_fc2: bfloat16 [4096, 1024], P('row', 'col'), may hold values from -0.09375 to 0.09375
- ln1_gain: bfloat16 [1024], P(('col', 'row')), may hold values from 0.099609375 to 1.8984375
- ln1_bias: bfloat16 [1024], P(('col', 'row')), may hold values from -6 to 6
- q_bias: bfloat16 [1024], P(('col', 'row')), may hold values from -6 to 6
- v_bias: bfloat16 [1024], P(('col', 'row')), may hold values from -0.4375 to 0.4375
- proj_bias: bfloat16 [1024], P(('col', 'row')), may hold values from -6 to 6
- ln2_gain: bfloat16 [1024], P(('col', 'row')), may hold values from 0.099609375 to 1.8984375
- ln2_bias: bfloat16 [1024], P(('col', 'row')), may hold values from -6 to 6
- fc1_bias: bfloat16 [4096], P(('col', 'row')), may hold values from -6 to 6
- fc2_bias: bfloat16 [1024], P(('col', 'row')), may hold values from -6 to 6
- cotangent: float32 [25088, 1024], P(('col', 'row')), may hold values from -6 to 6
Outputs:
- output: bfloat16 [25088, 1024], P(('col', 'row'))
- grad_tokens: float32 [25088, 1024], P(('col', 'row'))
- grad_qkv: float32 [1024, 3072], P('row', 'col')
- grad_proj: float32 [1024, 1024], P('row', 'col')
- grad_fc1: float32 [1024, 4096], P('row', 'col')
- grad_fc2: float32 [4096, 1024], P('row', 'col')
- grad_ln1_gain: float32 [1024], P(('col', 'row'))
- grad_ln1_bias: float32 [1024], P(('col', 'row'))
- grad_q_bias: float32 [1024], P(('col', 'row'))
- grad_v_bias: float32 [1024], P(('col', 'row'))
- grad_proj_bias: float32 [1024], P(('col', 'row'))
- grad_ln2_gain: float32 [1024], P(('col', 'row'))
- grad_ln2_bias: float32 [1024], P(('col', 'row'))
- grad_fc1_bias: float32 [4096], P(('col', 'row'))
- grad_fc2_bias: float32 [1024], P(('col', 'row'))
All inputs are finite; a program needn't handle non-finite values.
Results may differ from a plain program's by a relative error of at most 0.019.
Values may be sent and summed in bfloat16 or wider, within the bound.
No kernel may reach another device: no remote copies, remote signals or barrier semaphores. Data moves between devices by JAX's collectives and lax.ppermute only.
A program may use at most 448 MiB of HBM per device.

v0:
```python
import math
import jax
import jax.numpy as jnp
from jax import lax
from jax.sharding import PartitionSpec as P

D = 1024
H = 16
HD = 64
LEN = 1568
EPSILON = 1e-06


def layer_norm(value, gain, shift):
    average = jnp.mean(value, axis=-1, keepdims=True)
    centred = value - average
    spread = jnp.mean(centred * centred, axis=-1, keepdims=True)
    inverse = lax.rsqrt(spread + EPSILON)
    normed = centred * inverse
    return (normed * gain + shift, normed, inverse)


def norm_back(grad_out, normed, inverse, gain):
    scaled = grad_out * gain
    mean_first = jnp.mean(scaled, axis=-1, keepdims=True)
    mean_second = jnp.mean(scaled * normed, axis=-1, keepdims=True)
    return inverse * (scaled - mean_first - normed * mean_second)


def gelu_slope(pre_act):
    cumulative = 0.5 * (1.0 + lax.erf(pre_act * 2.0 ** (-0.5)))
    density = jnp.exp(-0.5 * pre_act * pre_act) * (2.0 * math.pi) ** (-0.5)
    return cumulative + pre_act * density


def inner_rows(first, second):
    return lax.dot_general(
        first, second, (((0,), (0,)), ((), ())), preferred_element_type=jnp.float32
    )


def outer_cols(first, second):
    return lax.dot_general(
        first, second, (((1,), (1,)), ((), ())), preferred_element_type=jnp.float32
    )


def clip_forward(block):
    queries, key_rows, value_rows = (block[:, 0], block[:, 1], block[:, 2])
    scores = jnp.einsum(
        "qhd,khd->hqk", queries, key_rows, preferred_element_type=jnp.float32
    ) * HD ** (-0.5)
    row_peak = jnp.max(scores, axis=-1, keepdims=True)
    exponent = jnp.exp(scores - row_peak)
    row_total = jnp.sum(exponent, axis=-1, keepdims=True)
    weights_low = (exponent / row_total).astype(jnp.bfloat16)
    mixed_heads = jnp.einsum(
        "hqk,khd->qhd", weights_low, value_rows, preferred_element_type=jnp.float32
    )
    return (mixed_heads.astype(jnp.bfloat16), (row_peak + jnp.log(row_total))[..., 0])


def clip_backward(element):
    block, grad_mixed, logsum = element
    queries, key_rows, value_rows = (block[:, 0], block[:, 1], block[:, 2])
    scores = jnp.einsum(
        "qhd,khd->hqk", queries, key_rows, preferred_element_type=jnp.float32
    ) * HD ** (-0.5)
    weights_full = jnp.exp(scores - logsum[..., None])
    weights_low = weights_full.astype(jnp.bfloat16)
    grad_values = jnp.einsum(
        "hqk,qhd->khd", weights_low, grad_mixed, preferred_element_type=jnp.float32
    )
    grad_weights = jnp.einsum(
        "qhd,khd->hqk", grad_mixed, value_rows, preferred_element_type=jnp.float32
    )
    row_delta = jnp.sum(grad_weights * weights_full, axis=-1, keepdims=True)
    grad_scores = (weights_full * (grad_weights - row_delta)).astype(jnp.bfloat16)
    grad_queries = jnp.einsum(
        "hqk,khd->qhd", grad_scores, key_rows, preferred_element_type=jnp.float32
    ) * HD ** (-0.5)
    grad_keys = jnp.einsum(
        "hqk,qhd->khd", grad_scores, queries, preferred_element_type=jnp.float32
    ) * HD ** (-0.5)
    return jnp.stack([grad_queries, grad_keys, grad_values], axis=1).astype(jnp.bfloat16)


def per_device(
    tokens,
    w_qkv,
    w_proj,
    w_fc1,
    w_fc2,
    ln1_gain,
    ln1_bias,
    q_bias,
    v_bias,
    proj_bias,
    ln2_gain,
    ln2_bias,
    fc1_bias,
    fc2_bias,
    cotangent,
):
    (
        qkv_part,
        proj_part,
        fc1_part,
        fc2_part,
        gain1_part,
        shift1_part,
        biasq_part,
        biasv_part,
        biasp_part,
        gain2_part,
        shift2_part,
        bias1_part,
        bias2_part,
    ) = (
        lax.all_gather(w_qkv, "row", axis=0, tiled=True),
        lax.all_gather(w_proj, "row", axis=0, tiled=True),
        lax.all_gather(w_fc1, "row", axis=0, tiled=True),
        lax.all_gather(w_fc2, "row", axis=0, tiled=True),
        lax.all_gather(ln1_gain, "row", axis=0, tiled=True),
        lax.all_gather(ln1_bias, "row", axis=0, tiled=True),
        lax.all_gather(q_bias, "row", axis=0, tiled=True),
        lax.all_gather(v_bias, "row", axis=0, tiled=True),
        lax.all_gather(proj_bias, "row", axis=0, tiled=True),
        lax.all_gather(ln2_gain, "row", axis=0, tiled=True),
        lax.all_gather(ln2_bias, "row", axis=0, tiled=True),
        lax.all_gather(fc1_bias, "row", axis=0, tiled=True),
        lax.all_gather(fc2_bias, "row", axis=0, tiled=True),
    )
    (
        full_qkv,
        full_proj,
        full_fc1,
        full_fc2,
        full_gain1,
        full_shift1,
        full_biasq,
        full_biasv,
        full_biasp,
        full_gain2,
        full_shift2,
        full_bias1,
        full_bias2,
    ) = (
        lax.all_gather(qkv_part, "col", axis=1, tiled=True),
        lax.all_gather(proj_part, "col", axis=1, tiled=True),
        lax.all_gather(fc1_part, "col", axis=1, tiled=True),
        lax.all_gather(fc2_part, "col", axis=1, tiled=True),
        lax.all_gather(gain1_part, "col", axis=0, tiled=True),
        lax.all_gather(shift1_part, "col", axis=0, tiled=True),
        lax.all_gather(biasq_part, "col", axis=0, tiled=True),
        lax.all_gather(biasv_part, "col", axis=0, tiled=True),
        lax.all_gather(biasp_part, "col", axis=0, tiled=True),
        lax.all_gather(gain2_part, "col", axis=0, tiled=True),
        lax.all_gather(shift2_part, "col", axis=0, tiled=True),
        lax.all_gather(bias1_part, "col", axis=0, tiled=True),
        lax.all_gather(bias2_part, "col", axis=0, tiled=True),
    )
    gain_first = full_gain1.astype(jnp.float32)
    gain_second = full_gain2.astype(jnp.float32)
    groups = lax.axis_size("row")
    heads_local = H // groups
    per_group = heads_local * HD
    inputs = tokens.astype(jnp.float32)
    token_rows = inputs.shape[0]
    normed_out1, normed_one, inverse_one = layer_norm(
        inputs, gain_first, full_shift1.astype(jnp.float32)
    )
    hidden_one = normed_out1.astype(jnp.bfloat16)
    bias_q = full_biasq.astype(jnp.float32)
    qkv_bias = jnp.concatenate([bias_q, jnp.zeros_like(bias_q), full_biasv.astype(jnp.float32)])
    projected = jnp.dot(hidden_one, full_qkv, preferred_element_type=jnp.float32) + qkv_bias
    qkv_low = projected.astype(jnp.bfloat16).reshape(token_rows, 3, groups, per_group)
    by_heads = lax.all_to_all(qkv_low, "row", split_axis=2, concat_axis=0, tiled=True)
    col_rows = by_heads.shape[0]
    clip_count = col_rows // LEN
    blocks = by_heads.reshape(clip_count, LEN, 3, heads_local, HD)
    mixed_heads, logsum = lax.map(clip_forward, blocks)
    attended = lax.all_to_all(
        mixed_heads.reshape(col_rows, 1, per_group), "row", split_axis=0, concat_axis=1, tiled=True
    ).reshape(token_rows, D)
    middle = inputs + (
        jnp.dot(attended, full_proj, preferred_element_type=jnp.float32)
        + full_biasp.astype(jnp.float32)
    )
    normed_out2, normed_two, inverse_two = layer_norm(
        middle, gain_second, full_shift2.astype(jnp.float32)
    )
    hidden_two = normed_out2.astype(jnp.bfloat16)
    pre_act = jnp.dot(hidden_two, full_fc1, preferred_element_type=jnp.float32) + full_bias1.astype(
        jnp.float32
    )
    activated = jax.nn.gelu(pre_act, approximate=False).astype(jnp.bfloat16)
    result = middle + (
        jnp.dot(activated, full_fc2, preferred_element_type=jnp.float32)
        + full_bias2.astype(jnp.float32)
    )
    qkv_again, proj_again, fc1_again, fc2_again = (
        lax.all_gather(w_qkv, "row", axis=0, tiled=True),
        lax.all_gather(w_proj, "row", axis=0, tiled=True),
        lax.all_gather(w_fc1, "row", axis=0, tiled=True),
        lax.all_gather(w_fc2, "row", axis=0, tiled=True),
    )
    back_qkv, back_proj, back_fc1, back_fc2 = (
        lax.all_gather(qkv_again, "col", axis=1, tiled=True),
        lax.all_gather(proj_again, "col", axis=1, tiled=True),
        lax.all_gather(fc1_again, "col", axis=1, tiled=True),
        lax.all_gather(fc2_again, "col", axis=1, tiled=True),
    )
    grad_out = cotangent.astype(jnp.bfloat16)
    grad_bias2 = jnp.sum(grad_out.astype(jnp.float32), axis=0)
    grad_fc2 = inner_rows(activated, grad_out)
    grad_act = outer_cols(grad_out, back_fc2)
    grad_pre = (grad_act * gelu_slope(pre_act)).astype(jnp.bfloat16)
    grad_bias1 = jnp.sum(grad_pre.astype(jnp.float32), axis=0)
    grad_fc1 = inner_rows(hidden_two, grad_pre)
    grad_hidden2 = outer_cols(grad_pre, back_fc1)
    grad_gain2 = jnp.sum(grad_hidden2 * normed_two, axis=0)
    grad_shift2 = jnp.sum(grad_hidden2, axis=0)
    grad_middle = cotangent + norm_back(grad_hidden2, normed_two, inverse_two, gain_second)
    grad_branch = grad_middle.astype(jnp.bfloat16)
    grad_biasp = jnp.sum(grad_branch.astype(jnp.float32), axis=0)
    grad_proj = inner_rows(attended, grad_branch)
    grad_attended = outer_cols(grad_branch, back_proj).astype(jnp.bfloat16)
    grad_heads = lax.all_to_all(
        grad_attended.reshape(token_rows, groups, per_group),
        "row",
        split_axis=1,
        concat_axis=0,
        tiled=True,
    )
    grad_blocks = grad_heads.reshape(clip_count, LEN, heads_local, HD)
    grad_triple = lax.map(clip_backward, (blocks, grad_blocks, logsum))
    grad_tokens_qkv = lax.all_to_all(
        grad_triple.reshape(col_rows, 3, 1, per_group),
        "row",
        split_axis=0,
        concat_axis=2,
        tiled=True,
    ).reshape(token_rows, 3 * D)
    grad_qkv_float = grad_tokens_qkv.astype(jnp.float32)
    grad_biasq = jnp.sum(grad_qkv_float[:, :D], axis=0)
    grad_biasv = jnp.sum(grad_qkv_float[:, 2 * D :], axis=0)
    grad_qkv = inner_rows(hidden_one, grad_tokens_qkv)
    grad_hidden1 = outer_cols(grad_tokens_qkv, back_qkv)
    grad_gain1 = jnp.sum(grad_hidden1 * normed_one, axis=0)
    grad_shift1 = jnp.sum(grad_hidden1, axis=0)
    grad_inputs = grad_middle + norm_back(grad_hidden1, normed_one, inverse_one, gain_first)
    (
        sum_qkv,
        sum_proj,
        sum_fc1,
        sum_fc2,
        sum_gain1,
        sum_shift1,
        sum_biasq,
        sum_biasv,
        sum_biasp,
        sum_gain2,
        sum_shift2,
        sum_bias1,
        sum_bias2,
    ) = (
        lax.psum_scatter(
            grad_qkv.astype(jnp.bfloat16), "col", scatter_dimension=1, tiled=True
        ).astype(jnp.float32),
        lax.psum_scatter(
            grad_proj.astype(jnp.bfloat16), "col", scatter_dimension=1, tiled=True
        ).astype(jnp.float32),
        lax.psum_scatter(
            grad_fc1.astype(jnp.bfloat16), "col", scatter_dimension=1, tiled=True
        ).astype(jnp.float32),
        lax.psum_scatter(
            grad_fc2.astype(jnp.bfloat16), "col", scatter_dimension=1, tiled=True
        ).astype(jnp.float32),
        lax.psum_scatter(
            grad_gain1.astype(jnp.bfloat16), "col", scatter_dimension=0, tiled=True
        ).astype(jnp.float32),
        lax.psum_scatter(
            grad_shift1.astype(jnp.bfloat16), "col", scatter_dimension=0, tiled=True
        ).astype(jnp.float32),
        lax.psum_scatter(
            grad_biasq.astype(jnp.bfloat16), "col", scatter_dimension=0, tiled=True
        ).astype(jnp.float32),
        lax.psum_scatter(
            grad_biasv.astype(jnp.bfloat16), "col", scatter_dimension=0, tiled=True
        ).astype(jnp.float32),
        lax.psum_scatter(
            grad_biasp.astype(jnp.bfloat16), "col", scatter_dimension=0, tiled=True
        ).astype(jnp.float32),
        lax.psum_scatter(
            grad_gain2.astype(jnp.bfloat16), "col", scatter_dimension=0, tiled=True
        ).astype(jnp.float32),
        lax.psum_scatter(
            grad_shift2.astype(jnp.bfloat16), "col", scatter_dimension=0, tiled=True
        ).astype(jnp.float32),
        lax.psum_scatter(
            grad_bias1.astype(jnp.bfloat16), "col", scatter_dimension=0, tiled=True
        ).astype(jnp.float32),
        lax.psum_scatter(
            grad_bias2.astype(jnp.bfloat16), "col", scatter_dimension=0, tiled=True
        ).astype(jnp.float32),
    )
    (
        out_qkv,
        out_proj,
        out_fc1,
        out_fc2,
        out_gain1,
        out_shift1,
        out_biasq,
        out_biasv,
        out_biasp,
        out_gain2,
        out_shift2,
        out_bias1,
        out_bias2,
    ) = (
        lax.psum_scatter(
            sum_qkv.astype(jnp.bfloat16), "row", scatter_dimension=0, tiled=True
        ).astype(jnp.float32),
        lax.psum_scatter(
            sum_proj.astype(jnp.bfloat16), "row", scatter_dimension=0, tiled=True
        ).astype(jnp.float32),
        lax.psum_scatter(
            sum_fc1.astype(jnp.bfloat16), "row", scatter_dimension=0, tiled=True
        ).astype(jnp.float32),
        lax.psum_scatter(
            sum_fc2.astype(jnp.bfloat16), "row", scatter_dimension=0, tiled=True
        ).astype(jnp.float32),
        lax.psum_scatter(
            sum_gain1.astype(jnp.bfloat16), "row", scatter_dimension=0, tiled=True
        ).astype(jnp.float32),
        lax.psum_scatter(
            sum_shift1.astype(jnp.bfloat16), "row", scatter_dimension=0, tiled=True
        ).astype(jnp.float32),
        lax.psum_scatter(
            sum_biasq.astype(jnp.bfloat16), "row", scatter_dimension=0, tiled=True
        ).astype(jnp.float32),
        lax.psum_scatter(
            sum_biasv.astype(jnp.bfloat16), "row", scatter_dimension=0, tiled=True
        ).astype(jnp.float32),
        lax.psum_scatter(
            sum_biasp.astype(jnp.bfloat16), "row", scatter_dimension=0, tiled=True
        ).astype(jnp.float32),
        lax.psum_scatter(
            sum_gain2.astype(jnp.bfloat16), "row", scatter_dimension=0, tiled=True
        ).astype(jnp.float32),
        lax.psum_scatter(
            sum_shift2.astype(jnp.bfloat16), "row", scatter_dimension=0, tiled=True
        ).astype(jnp.float32),
        lax.psum_scatter(
            sum_bias1.astype(jnp.bfloat16), "row", scatter_dimension=0, tiled=True
        ).astype(jnp.float32),
        lax.psum_scatter(
            sum_bias2.astype(jnp.bfloat16), "row", scatter_dimension=0, tiled=True
        ).astype(jnp.float32),
    )
    return (
        result.astype(jnp.bfloat16),
        grad_inputs,
        out_qkv,
        out_proj,
        out_fc1,
        out_fc2,
        out_gain1,
        out_shift1,
        out_biasq,
        out_biasv,
        out_biasp,
        out_gain2,
        out_shift2,
        out_bias1,
        out_bias2,
    )


def solution(mesh):
    return jax.shard_map(
        per_device,
        mesh=mesh,
        in_specs=(
            P(("col", "row"), None),
            P("row", "col"),
            P("row", "col"),
            P("row", "col"),
            P("row", "col"),
            P(("col", "row")),
            P(("col", "row")),
            P(("col", "row")),
            P(("col", "row")),
            P(("col", "row")),
            P(("col", "row")),
            P(("col", "row")),
            P(("col", "row")),
            P(("col", "row")),
            P(("col", "row"), None),
        ),
        out_specs=(
            P(("col", "row"), None),
            P(("col", "row"), None),
            P("row", "col"),
            P("row", "col"),
            P("row", "col"),
            P("row", "col"),
            P(("col", "row")),
            P(("col", "row")),
            P(("col", "row")),
            P(("col", "row")),
            P(("col", "row")),
            P(("col", "row")),
            P(("col", "row")),
            P(("col", "row")),
            P(("col", "row")),
        ),
        check_vma=False,
    )
```

profile of v0, /device:TPU:0, one launch (start us, length us, event | category | flops | bytes accessed | tf_op | source)
XLA Modules:
  0.0 1200.0 jit_solution(12227109749676747950)
XLA Ops:
  7.2 10.6 all_gather.90
  17.9 5.2 all_gather.96
  23.2 8.9 all_gather.104
  41.6 5.4 all-reduce.37
  48.5 59.9 %all-reduce.35 = (bf16[1024]{0:T(1024)(128)(2,1)S(1)}, bf16[1024]{0:T(1024)(128)(2,1)S(1)}, bf16[1024]{0:T(1024)(128)(2,1)S(1)}, bf16[1024]{0:T(1024)(128)(2,1)S...) all-reduce(bf16[1024]{0:T(1024)(128)(2,1)S(1)} %dynamic-update-slic, ...), channel_id=1, replica_groups=mesh['row'=2,'col'=16] {'col'}, use_global_device_ids=true, to_apply=%add.7 | all-reduce | flops 7168 | bytes 28672
  110.8 10.2 add_convert_fusion
  120.9 12.0 reshape.168
  132.9 5.4 copy.48
  138.3 6.0 all-to-all-start
  144.3 55.4 %all_gather.108 = bf16[4096,64]{0,1:T(8,128)(2,1)} all-gather(bf16[2048,64]{0,1:T(8,128)(2,1)S(1)} %copy-done.11), channel_id=1, replica_groups=mesh['row'=2,'col'=16] {'row'}, dimensions={0}, use_global_device_ids=true | all-gather | bytes 786432 | tf_op jit(solution)/shard_map/all_gather | solution.py:123
  199.7 14.2 %copy.49 = bf16[2,784,3,1,512]{1,0,4,2,3:T(2,128)(2,1)} copy(bf16[2,784,3,1,512]{4,1,2,0,3:T(8,128)(2,1)} %bitcast.3) | data formatting | bytes 9633792 | tf_op jit(solution)/shard_map/all_to_all | solution.py:178
  214.0 11.7 squeeze.35
  225.7 32.2 %multiply_reduce_fusion.1 = (f32[8,1568]{1,0:T(8,128)S(1)}, f32[8,1568,1568]{1,2,0:T(8,128)}) fusion(bf16[1568,3,8,64]{0,3,2,1:T(8,128)(2,1)} %squeeze.35), kind=kOutput, calls=%fused_computation.6 | convolution fusion | flops 2556956416 | bytes 82134016 | tf_op jit(solution)/shard_map/while/body/eval_jaxpr/qhd,khd->hqk/dot_general | solution.py:50
  257.9 26.7 %fusion = f32[8,1568]{1,0:T(8,128)S(1)} fusion(f32[8,1568,1568]{1,2,0:T(8,128)} %get-tuple-element.94, f32[8,1568]{1,0:T(8,128)S(1)} %get-tuple-element.93), kind=kLoop, calls=%fused_computation.5 | loop fusion | flops 58994432 | bytes 78776320 | tf_op jit(solution)/shard_map/while/body/eval_jaxpr/reduce_sum | solution.py:55
  284.7 30.8 %fusion.38 = bf16[8,64,1568]{2,1,0:T(8,128)(2,1)S(1)} fusion(f32[8,1568,1568]{1,2,0:T(8,128)} %get-tuple-element.94, f32[8,1568]{1,0:T(8,128)S(1)} %fusion, f32[8,1568]{1,0:T(8,128)S(1)} %get-tuple-element.93, bf16[1568,3,8,64]{0,3,2,1:T(8,128)(2,1)} %squeeze.35), kind=kOutput, calls=%fused_computation.70 | convolution fusion | flops 2597109760 | bytes 86902784 | tf_op jit(solution)/shard_map/while/body/eval_jaxpr/hqk,khd->qhd/dot_general | solution.py:57
  316.0 1.9 reduce.3
  319.4 2.1 reshape.277
  321.5 3.7 all-to-all-start.1
  325.2 14.5 %all-gather = bf16[2,1,128]{2,1,0:T(2,128)(2,1)S(1)} all-gather(bf16[1,1,128]{2,1,0:T(2,128)(2,1)S(1)} %bitcast.100), channel_id=1, replica_groups=mesh['row'=2,'col'=16] {'row'}, dimensions={0}, use_global_device_ids=true | all-gather | bytes 768 | tf_op jit(solution)/shard_map/all_gather | solution.py:131
  339.7 25.8 %all-gather.1 = bf16[16,1,256]{2,1,0:T(2,128)(2,1)S(1)} all-gather(bf16[1,1,256]{2,1,0:T(2,128)(2,1)S(1)} %bitcast.99), channel_id=1, replica_groups=mesh['row'=2,'col'=16] {'col'}, dimensions={0}, use_global_device_ids=true | all-gather | bytes 8704 | tf_op jit(solution)/shard_map/all_gather | solution.py:160
  365.5 2.5 reshape.278
  368.1 2.5 copy.67
  372.7 4.1 fusion.52
  379.1 39.0 %fusion.7 = (bf16[784,4096]{1,0:T(8,128)(2,1)}, f32[784,4096]{1,0:T(8,128)}) fusion(f32[4096]{0:T(1024)S(1)} %bitcast.97, bf16[1024,4096]{1,0:T(8,128)(2,1)} %all-gather.11.cloned.1.call-done, f32[784,1024]{1,0:T(8,128)} %copy-done.5, f32[1024]{0:T(1024)S(1)} %convert_element_type.201, f32[1024]{0:T(1024)S(1)} %convert_element_type.200, ...), kind=kOutput, calls=%fused_computation.14 | convolution fusion | flops 6792626176 | bytes 30898304 | tf_op jit(solution)/shard_map/dot_general | solution.py:194
  418.1 17.1 %fusion.53 = (bf16[4096]{0:T(1024)(128)(2,1)}, bf16[784,4096]{1,0:T(8,128)(2,1)}) fusion(f32[784,4096]{1,0:T(8,128)} %get-tuple-element.104, f32[4096]{0:T(1024)S(1)} %bitcast.98, bf16[4096,1024]{0,1:T(8,128)(2,1)} %all-gather.13.cloned.1.call-done, f32[784,1024]{1,0:T(8,128)S(1)} %copy-done.7), kind=kOutput, calls=%fused_computation.112 | convolution fusion | flops 6616002560 | bytes 30892032 | tf_op jit(solution)/shard_map/dot_general | solution.py:43
  435.2 11.0 multiply_reduce_fusion.2
  446.3 2.0 convert_reduce_fusion.1
  448.3 1.8 convolution_convert_fusion.4
  451.4 3.7 all-to-all-start.2
  455.1 20.3 %all-to-all-done.2 = bf16[784,2,512]{2,0,1:T(8,128)(2,1)S(1)} async-done(((bf16[784,2,512]{2,0,1:T(8,128)(2,1)}), bf16[784,2,512]{2,0,1:T(8,128)(2,1)S(1)}, u32[]{:S(2)}, u32[]{:S(2)}) %all-to-all-start.2) | async-done | bytes 1605664 | tf_op jit(solution)/shard_map/all_to_all | solution.py:229
  475.4 4.0 copy.54
  479.4 4.0 squeeze.39
  483.4 29.4 %fusion.35 = bf16[8,64,1568]{2,1,0:T(8,128)(2,1)} fusion(bf16[1568,8,64]{0,2,1:T(8,128)(2,1)S(1)} %squeeze.39, f32[8,1568,1568]{1,2,0:T(8,128)} %get-tuple-element.94, f32[8,1568]{1,0:T(8,128)S(1)} %log_add_fusion), kind=kOutput, calls=%fused_computation.69 | convolution fusion | flops 2577440768 | bytes 81937408 | tf_op jit(solution)/shard_map/while/body/eval_jaxpr/hqk,qhd->khd/dot_general | solution.py:71
  512.9 56.6 %multiply_reduce_fusion = (f32[8,1568]{1,0:T(8,128)S(1)}, f32[8,1568,1568]{1,2,0:T(8,128)}) fusion(f32[8,1568,1568]{1,2,0:T(8,128)} %get-tuple-element.94, f32[8,1568]{1,0:T(8,128)S(1)} %log_add_fusion, bf16[1568,8,64]{0,2,1:T(8,128)(2,1)S(1)} %squeeze.39, bf16[1568,3,8,64]{0,3,2,1:T(8,128)(2,1)} %squeeze.35), kind=kOutput, calls=%fused_computation.1 | convolution fusion | flops 2596294400 | bytes 165578752 | tf_op jit(solution)/shard_map/while/body/eval_jaxpr/qhd,khd->hqk/dot_general | solution.py:74
  569.5 64.8 %multiply_convert_fusion = bf16[8,1568,1568]{1,2,0:T(8,128)(2,1)} fusion(f32[8,1568,1568]{1,2,0:T(8,128)} %get-tuple-element.99, f32[8,1568,1568]{1,2,0:T(8,128)} %get-tuple-element.94, f32[8,1568]{1,0:T(8,128)S(1)} %get-tuple-element.98, f32[8,1568]{1,0:T(8,128)S(1)} %log_add_fusion), kind=kLoop, calls=%fused_computation | loop fusion | flops 98344960 | bytes 196790272 | tf_op jit(solution)/shard_map/while/body/eval_jaxpr/convert_element_type | solution.py:78
  634.3 20.6 %multiply_convert_fusion.1 = bf16[8,64,1568]{2,1,0:T(8,128)(2,1)} fusion(bf16[8,1568,1568]{1,2,0:T(8,128)(2,1)} %multiply_convert_fusion, bf16[1568,3,8,64]{0,3,2,1:T(8,128)(2,1)} %squeeze.35), kind=kOutput, calls=%fused_computation.50 | convolution fusion | flops 2519236608 | bytes 45056000 | tf_op jit(solution)/shard_map/while/body/eval_jaxpr/hqk,qhd->khd/dot_general | solution.py:82
  654.9 21.0 %multiply_convert_fusion.2 = bf16[8,64,1568]{2,1,0:T(8,128)(2,1)} fusion(bf16[8,1568,1568]{1,2,0:T(8,128)(2,1)} %multiply_convert_fusion, bf16[1568,3,8,64]{0,3,2,1:T(8,128)(2,1)} %squeeze.35), kind=kOutput, calls=%fused_computation.51 | convolution fusion | flops 2519236608 | bytes 45056000 | tf_op jit(solution)/shard_map/while/body/eval_jaxpr/hqk,khd->qhd/dot_general | solution.py:79
  675.9 9.1 copy.60
  685.0 8.7 copy.59
  693.7 8.7 copy.58
  702.5 13.9 %pad_maximum_fusion = bf16[1568,3,1,512]{3,1,2,0:T(4,128)(2,1)} fusion(bf16[1568,1,1,512]{3,1,2,0:T(2,128)(2,1)S(1)} %copy.60, bf16[1568,1,1,512]{3,1,2,0:T(2,128)(2,1)} %copy.59, bf16[1568,1,1,512]{3,1,2,0:T(2,128)(2,1)} %copy.58), kind=kLoop, calls=%fused_computation.39 | loop fusion | flops 14450688 | bytes 9633792 | tf_op jit(solution)/shard_map/while/body/eval_jaxpr/stack | solution.py:85
  716.4 6.7 all-to-all-start.3
  723.1 5.1 convolution_convert_fusion.3
  728.4 65.8 %all-to-all-done.3 = bf16[1568,3,1,512]{3,1,2,0:T(4,128)(2,1)} async-done(((bf16[1568,3,1,512]{3,1,2,0:T(4,128)(2,1)}), bf16[1568,3,1,512]{3,1,2,0:T(4,128)(2,1)}, u32[]{:S(2)}, u32[]{:S(2)}) %all-to-all-start.3) | async-done | bytes 4816928 | tf_op jit(solution)/shard_map/all_to_all | solution.py:238
  794.2 6.2 copy.61
  800.4 9.5 copy.62
  810.0 12.2 %reshape.172 = bf16[784,3072]{1,0:T(8,128)(2,1)} reshape(bf16[784,3,2,1,512]{4,2,1,0,3:T(2,128)(2,1)} %copy.62) | data formatting | bytes 9633792 | tf_op jit(solution)/shard_map/reshape | solution.py:244
  822.2 11.4 convolution_convert_fusion.2
  834.3 15.0 %convolution_convert_fusion.1 = bf16[1024,4096]{1,0:T(8,128)(2,1)} fusion(bf16[784,4096]{1,0:T(8,128)(2,1)} %get-tuple-element.102, f32[784,1024]{1,0:T(8,128)} %copy-done.5, f32[1024]{0:T(1024)S(1)} %copy-done.32, f32[1024]{0:T(1024)S(1)} %copy-done.23, f32[784]{0:T(1024)S(1)} %copy-done.25, f32[784]{0:T(1024)S(1)} %copy-done.17), kind=kOutput, calls=%fused_computation.38 | convolution fusion | flops 6584877056 | bytes 18036864 | tf_op jit(solution)/shard_map/dot_general | solution.py:37
  849.3 14.9 %convolution_convert_fusion = bf16[4096,1024]{0,1:T(8,128)(2,1)} fusion(bf16[784,4096]{1,0:T(8,128)(2,1)} %get-tuple-element.103, f32[784,1024]{1,0:T(8,128)} %param.29), kind=kOutput, calls=%fused_computation.37 | convolution fusion | flops 6581665792 | bytes 18022400 | tf_op jit(solution)/shard_map/dot_general | solution.py:37
  867.9 47.0 %reduce-scatter.9.cloned.1.call-done = bf16[1024,192]{0,1:T(8,128)(2,1)} async-done(((bf16[1024,3072]{0,1:T(8,128)(2,1)}), bf16[1024,192]{0,1:T(8,128)(2,1)}) %reduce-scatter.9.cloned.1.call-update) | async-done | bytes 393232 | tf_op jit(solution)/shard_map/reduce_scatter | solution.py:268
  915.0 10.5 fusion.33
  925.5 4.1 convert_element_type.225
  930.3 61.4 %all-reduce.34 = (bf16[1024]{0:T(1024)(128)(2,1)S(1)}, bf16[1024]{0:T(1024)(128)(2,1)S(1)}, bf16[1024]{0:T(1024)(128)(2,1)S(1)}, bf16[1024]{0:T(1024)(128)(2,1)S...) all-reduce(bf16[1024]{0:T(1024)(128)(2,1)S(1)} %dynamic-update-slic, ...), channel_id=1, replica_groups=mesh['row'=2,'col'=16] {'col'}, use_global_device_ids=true, to_apply=%add.15 | all-reduce | flops 13312 | bytes 53248
  991.7 30.7 %reduce-scatter.17.cloned.1.call-done = bf16[1024,256]{1,0:T(8,128)(2,1)} async-done(((bf16[1024,4096]{1,0:T(8,128)(2,1)}), bf16[1024,256]{1,0:T(8,128)(2,1)}) %reduce-scatter.17.cloned.1.call-update) | async-done | bytes 524304 | tf_op jit(solution)/shard_map/reduce_scatter | solution.py:274
  1022.5 12.5 %add_convert_fusion.1 = bf16[784,1024]{1,0:T(8,128)(2,1)} fusion(f32[784,1024]{1,0:T(8,128)} %copy-done.5, f32[1024]{0:T(1024)S(1)} %convert_element_type.205, bf16[784,4096]{1,0:T(8,128)(2,1)} %get-tuple-element.103, bf16[4096,1024]{0,1:T(8,128)(2,1)} %all-gather.13.cloned.1.call-done), kind=kOutput, calls=%fused_computation.65 | convolution fusion | flops 6579077120 | bytes 19632128 | tf_op jit(solution)/shard_map/dot_general | solution.py:199
  1035.7 5.0 all-reduce.36
  1045.3 84.3 %reduce-scatter.21.cloned.1.call-done = bf16[4096,64]{0,1:T(8,128)(2,1)} async-done(((bf16[4096,1024]{0,1:T(8,128)(2,1)}), bf16[4096,64]{0,1:T(8,128)(2,1)}) %reduce-scatter.21.cloned.1.call-update) | async-done | bytes 524304 | tf_op jit(solution)/shard_map/reduce_scatter | solution.py:277
  1130.2 4.6 fusion.32
  1134.8 7.1 reduce-scatter.15.cloned.1.call-done
  1143.4 13.8 %reduce-scatter.11.cloned.1.call-done = bf16[512,192]{0,1:T(8,128)(2,1)} async-done(((bf16[1024,192]{0,1:T(8,128)(2,1)}), bf16[512,192]{0,1:T(8,128)(2,1)}) %reduce-scatter.11.cloned.1.call-update) | async-done | bytes 196624 | tf_op jit(solution)/shard_map/reduce_scatter | solution.py:323
  1158.9 15.2 %reduce-scatter.19.cloned.1.call-done = bf16[512,256]{1,0:T(8,128)(2,1)} async-done(((bf16[1024,256]{1,0:T(8,128)(2,1)}), bf16[512,256]{1,0:T(8,128)(2,1)}) %reduce-scatter.19.cloned.1.call-update) | async-done | bytes 262160 | tf_op jit(solution)/shard_map/reduce_scatter | solution.py:329
  1175.9 15.0 %reduce-scatter.23.cloned.1.call-done = bf16[2048,64]{0,1:T(8,128)(2,1)} async-done(((bf16[4096,64]{0,1:T(8,128)(2,1)}), bf16[2048,64]{0,1:T(8,128)(2,1)}) %reduce-scatter.23.cloned.1.call-update) | async-done | bytes 262160 | tf_op jit(solution)/shard_map/reduce_scatter | solution.py:332
  1190.9 1.8 convert_element_type.220
  (198 shorter events, 33.4 us)
Async XLA Ops:
  7.2 102.9 %copy-start = (bf16[784,1024]{1,0:T(8,128)(2,1)S(1)}, bf16[784,1024]{1,0:T(8,128)(2,1)}, u32[]{:S(2)}) copy-start(bf16[784,1024]{1,0:T(8,128)(2,1)} %param.15) | copy-start | bytes 4816900
  7.2 103.6 %all-gather.7.cloned.1.call-start = ((), (), s32[]{:S(2)}) async-start(), calls=%async_computation.12 | async-start | bytes 6684672 | tf_op jit(solution)/shard_map/all_gather | solution.py:149
  17.9 354.8 %all-gather.9.cloned.1.call-start = ((), (), s32[]{:S(2)}) async-start(), calls=%async_computation.13 | async-start | bytes 2228224 | tf_op jit(solution)/shard_map/all_gather | solution.py:150
  23.2 355.8 %all-gather.11.cloned.1.call-start = ((), (), s32[]{:S(2)}) async-start(), calls=%async_computation.14 | async-start | bytes 8912896 | tf_op jit(solution)/shard_map/all_gather | solution.py:151
  108.3 12.6 %copy-start.18 = (f32[1024]{0:T(1024)}, f32[1024]{0:T(1024)S(1)}, u32[]{:S(2)}) copy-start(f32[1024]{0:T(1024)S(1)} %convert_element_type.190) | copy-start | bytes 12292
  108.3 12.6 %copy-start.29 = (f32[1024]{0:T(1024)}, f32[1024]{0:T(1024)S(1)}, u32[]{:S(2)}) copy-start(f32[1024]{0:T(1024)S(1)} %convert_element_type.191) | copy-start | bytes 12292
  110.1 10.8 copy-start.14
  110.7 10.2 copy-start.20
  138.3 6.0 copy-start.11
  138.3 61.4 %all-to-all-start = ((bf16[784,3,2,512]{3,0,1,2:T(8,128)(2,1)}), bf16[784,3,2,512]{3,0,1,2:T(8,128)(2,1)}, u32[]{:S(2)}, u32[]{:S(2)}) async-start(bf16[784,3,2,512]{3,0,1,2:T(8,128)(2,1)} %copy.48), calls=%async_computation | async-start | bytes 9633792 | tf_op jit(solution)/shard_map/all_to_all | solution.py:178
  144.3 273.8 %all-gather.13.cloned.1.call-start = ((), (), s32[]{:S(2)}) async-start(), calls=%async_computation.15 | async-start | bytes 8912896 | tf_op jit(solution)/shard_map/all_gather | solution.py:152
  257.9 26.7 %copy-start.9 = (f32[8,1568]{1,0:T(8,128)}, f32[8,1568]{1,0:T(8,128)S(1)}, u32[]{:S(2)}) copy-start(f32[8,1568]{1,0:T(8,128)S(1)} %get-tuple-element.93) | copy-start | bytes 150532
  284.7 30.8 %copy-start.12 = (f32[8,1568]{1,0:T(8,128)}, f32[8,1568]{1,0:T(8,128)S(1)}, u32[]{:S(2)}) copy-start(f32[8,1568]{1,0:T(8,128)S(1)} %fusion) | copy-start | bytes 150532
  318.0 7.2 copy-start.35
  318.0 7.2 copy-start.34
  318.0 7.2 copy-start.33
  318.0 7.2 copy-start.40
  321.5 44.1 %all-to-all-start.1 = ((bf16[2,2,200704]{2,1,0:T(2,128)(2,1)}), bf16[2,2,200704]{2,1,0:T(2,128)(2,1)S(1)}, u32[]{:S(2)}, u32[]{:S(2)}) async-start(bf16[2,2,200704]{2,1,0:T(2,128)(2,1)} %reshape.277), calls=%async_computation.1 | async-start | bytes 3211264 | tf_op jit(solution)/shard_map/all_to_all | solution.py:183
  325.2 121.1 %copy-start.22 = (f32[1024]{0:T(1024)}, f32[1024]{0:T(1024)S(1)}, u32[]{:S(2)}) copy-start(f32[1024]{0:T(1024)S(1)} %convert_element_type.200) | copy-start | bytes 12292
  325.2 53.9 %copy-start.31 = (f32[1024]{0:T(1024)}, f32[1024]{0:T(1024)S(1)}, u32[]{:S(2)}) copy-start(f32[1024]{0:T(1024)S(1)} %convert_element_type.201) | copy-start | bytes 12292
  368.1 4.6 copy-start.1
  372.6 4.2 copy-start.8
  376.8 1.7 copy-start.5
  376.9 69.4 %copy-start.16 = (f32[784]{0:T(1024)}, f32[784]{0:T(1024)S(1)}, u32[]{:S(2)}) copy-start(f32[784]{0:T(1024)S(1)} %broadcast_multiply_fusion.4) | copy-start | bytes 9412
  379.0 67.2 %copy-start.24 = (f32[784]{0:T(1024)}, f32[784]{0:T(1024)S(1)}, u32[]{:S(2)}) copy-start(f32[784]{0:T(1024)S(1)} %add_rsqrt_fusion) | copy-start | bytes 9412
  379.1 39.0 %copy-start.7 = (f32[784,1024]{1,0:T(8,128)S(1)}, f32[784,1024]{1,0:T(8,128)}, u32[]{:S(2)}) copy-start(f32[784,1024]{1,0:T(8,128)} %param.29) | copy-start | bytes 9633796
  418.0 17.2 %copy-start.6 = (f32[784,1024]{1,0:T(8,128)S(1)}, f32[784,1024]{1,0:T(8,128)}, u32[]{:S(2)}) copy-start(f32[784,1024]{1,0:T(8,128)} %copy-done.5) | copy-start | bytes 9633796
  418.1 17.2 %copy-start.38 = (bf16[1024,4096]{1,0:T(8,128)(2,1)S(1)}, bf16[1024,4096]{1,0:T(8,128)(2,1)}, u32[]{:S(2)}) copy-start(bf16[1024,4096]{1,0:T(8,128)(2,1)} %all-gather.11.cloned.1.call-done) | copy-start | bytes 25165828
  446.2 2.0 copy-start.39
  448.3 1.8 copy-start.3
  450.1 5.0 copy-start.10
  450.1 5.0 copy-start.13
  451.4 24.0 %all-to-all-start.2 = ((bf16[784,2,512]{2,0,1:T(8,128)(2,1)}), bf16[784,2,512]{2,0,1:T(8,128)(2,1)S(1)}, u32[]{:S(2)}, u32[]{:S(2)}) async-start(bf16[784,2,512]{2,0,1:T(8,128)(2,1)} %bitcast.85), calls=%async_computation.2 | async-start | bytes 3211264 | tf_op jit(solution)/shard_map/all_to_all | solution.py:229
  716.4 6.7 copy-start.4
  716.4 77.9 %all-to-all-start.3 = ((bf16[1568,3,1,512]{3,1,2,0:T(4,128)(2,1)}), bf16[1568,3,1,512]{3,1,2,0:T(4,128)(2,1)}, u32[]{:S(2)}, u32[]{:S(2)}) async-start(bf16[1568,3,1,512]{3,1,2,0:T(4,128)(2,1)} %pad_maximum_fusion), calls=%async_computation.3 | async-start | bytes 12845056 | tf_op jit(solution)/shard_map/all_to_all | solution.py:238
  723.0 141.3 %reduce-scatter.13.cloned.1.call-start = ((), (), s32[]{:S(2)}) async-start(), calls=%async_computation.18 | async-start | bytes 2228224 | tf_op jit(solution)/shard_map/reduce_scatter | solution.py:271
  728.2 186.7 %reduce-scatter.9.cloned.1.call-start = ((), (), s32[]{:S(2)}) async-start(), calls=%async_computation.16 | async-start | bytes 6684672 | tf_op jit(solution)/shard_map/reduce_scatter | solution.py:268
  810.0 12.2 %copy-start.2 = (bf16[784,1024]{1,0:T(8,128)(2,1)S(1)}, bf16[784,1024]{1,0:T(8,128)(2,1)}, u32[]{:S(2)}) copy-start(bf16[784,1024]{1,0:T(8,128)(2,1)} %param.15) | copy-start | bytes 4816900
  810.0 12.2 %copy-start.15 = (f32[784]{0:T(1024)S(1)}, f32[784]{0:T(1024)}, u32[]{:S(2)}) copy-start(f32[784]{0:T(1024)} %copy-done.14) | copy-start | bytes 9412
  810.0 12.2 %copy-start.19 = (f32[1024]{0:T(1024)S(1)}, f32[1024]{0:T(1024)}, u32[]{:S(2)}) copy-start(f32[1024]{0:T(1024)} %copy-done.18) | copy-start | bytes 12292
  810.0 12.2 %copy-start.21 = (f32[784]{0:T(1024)S(1)}, f32[784]{0:T(1024)}, u32[]{:S(2)}) copy-start(f32[784]{0:T(1024)} %copy-done.20) | copy-start | bytes 9412
  810.0 12.2 %copy-start.30 = (f32[1024]{0:T(1024)S(1)}, f32[1024]{0:T(1024)}, u32[]{:S(2)}) copy-start(f32[1024]{0:T(1024)} %copy-done.29) | copy-start | bytes 12292
  833.6 0.7 copy-start.17
  833.6 0.7 copy-start.23
  833.6 0.7 copy-start.25
  833.6 0.7 copy-start.32
  833.6 188.8 %reduce-scatter.17.cloned.1.call-start = ((), (), s32[]{:S(2)}) async-start(), calls=%async_computation.20 | async-start | bytes 8912896 | tf_op jit(solution)/shard_map/reduce_scatter | solution.py:274
  849.3 280.4 %reduce-scatter.21.cloned.1.call-start = ((), (), s32[]{:S(2)}) async-start(), calls=%async_computation.22 | async-start | bytes 8912896 | tf_op jit(solution)/shard_map/reduce_scatter | solution.py:277
  864.2 3.4 copy-start.41
  864.3 277.6 %reduce-scatter.15.cloned.1.call-start = ((), (), s32[]{:S(2)}) async-start(), calls=%async_computation.19 | async-start | bytes 196608 | tf_op jit(solution)/shard_map/reduce_scatter | solution.py:326
  865.0 292.2 %reduce-scatter.11.cloned.1.call-start = ((), (), s32[]{:S(2)}) async-start(), calls=%async_computation.17 | async-start | bytes 589824 | tf_op jit(solution)/shard_map/reduce_scatter | solution.py:323
  914.9 259.2 %reduce-scatter.19.cloned.1.call-start = ((), (), s32[]{:S(2)}) async-start(), calls=%async_computation.21 | async-start | bytes 786432 | tf_op jit(solution)/shard_map/reduce_scatter | solution.py:329
  929.6 0.7 copy-start.26
  929.6 0.7 copy-start.27
  929.6 0.7 copy-start.28
  929.6 0.7 copy-start.36
  929.6 0.7 copy-start.37
  1022.4 168.5 %reduce-scatter.23.cloned.1.call-start = ((), (), s32[]{:S(2)}) async-start(), calls=%async_computation.23 | async-start | bytes 786432 | tf_op jit(solution)/shard_map/reduce_scatter | solution.py:332
Sparse Core Ops, SparseCore 0:
  18.0 62.1 all-gather.6
  82.3 40.4 all-gather.8
  125.0 76.2 all-gather.10
  203.3 72.4 all-gather.12
  728.3 59.4 reduce-scatter.12
  833.7 81.1 reduce-scatter.8
  919.0 103.3 reduce-scatter.16
  1026.5 103.1 reduce-scatter.20
  1131.8 10.0 reduce-scatter.14
  1144.0 13.1 reduce-scatter.10
  1159.5 14.6 reduce-scatter.18
  1176.2 14.6 reduce-scatter.22
where the time goes:
time: 1210 us; the launch traced here: 1200 us
  matrix products  343 us (28%)
  waiting for transfers between devices  300 us (25%)
  blocking collectives  252 us (21%)
  other arithmetic  133 us (11%)
  local copies, waits for them, and re-layouts  131 us (11%)
  starting transfers between devices  20.7 us (2%)
  between operations  19.3 us (2%)
    unnamed x4, blocking collectives  132 us
    reduce_scatter x1, waiting for transfers between devices, per_device(): lax.psum_scatter(grad_fc2.astype(jnp.bfloat16), 'col', scatter_dimension=...  84.3 us
    all_to_all x1, waiting for transfers between devices, per_device(): lax.all_to_all(grad_triple.reshape(col_rows, 3, 1, per_group), 'row', spl...  65.8 us
    convert_element_type x1, other arithmetic, clip_backward(): (weights_full * (grad_weights - row_delta)).astype(jnp.bfloat16)  64.8 us
    dot_general x1, matrix products, clip_backward(): jnp.einsum('qhd,khd->hqk', grad_mixed, value_rows, preferred_element_type...  56.6 us
    all_gather x1, blocking collectives, per_device(): lax.all_gather(w_fc2, 'row', axis=0, tiled=True)  55.4 us
    reduce_scatter x1, waiting for transfers between devices, per_device(): lax.psum_scatter(grad_qkv.astype(jnp.bfloat16), 'col', scatter_dimension=...  47 us
    dot_general x4, matrix products, inner_rows(): lax.dot_general(first, second, (((0,), (0,)), ((), ())), preferred_elemen...  46.4 us
  transfers between devices with their start and end apart: 16, of which 9 were waited for; matrix products, arithmetic and copies ran while one was open for 27% of the time, Pallas kernels for 0%

commit v1 on v0

--- a/solution.py
+++ b/solution.py
@@ -102,6 +102,13 @@
     fc2_bias,
     cotangent,
 ):
+
+    def lift_face(xx):
+        all_rows = jax.lax.axis_size("row")
+        fresh = jnp.split(xx, all_rows, 0)
+        moved = jax.lax.all_to_all(jnp.stack(fresh, 0), "row", 0, 0)
+        return jnp.concatenate(moved, 2)
+
     (
         qkv_part,
         proj_part,
@@ -235,13 +242,9 @@
     )
     grad_blocks = grad_heads.reshape(clip_count, LEN, heads_local, HD)
     grad_triple = lax.map(clip_backward, (blocks, grad_blocks, logsum))
-    grad_tokens_qkv = lax.all_to_all(
-        grad_triple.reshape(col_rows, 3, 1, per_group),
-        "row",
-        split_axis=0,
-        concat_axis=2,
-        tiled=True,
-    ).reshape(token_rows, 3 * D)
+    grad_tokens_qkv = lift_face(grad_triple.reshape(col_rows, 3, 1, per_group)).reshape(
+        token_rows, 3 * D
+    )
     grad_qkv_float = grad_tokens_qkv.astype(jnp.float32)
     grad_biasq = jnp.sum(grad_qkv_float[:, :D], axis=0)
     grad_biasv = jnp.sum(grad_qkv_float[:, 2 * D :], axis=0)

time: 1210 us -> 1160 us (0.959)
  local copies, waits for them, and re-layouts: 131 us -> 108 us
  waiting for transfers between devices: 300 us -> 282 us
    all_to_all x1, waiting for transfers between devices: 65.8 us -> 48.5 us  [lift_face(): moved = jax.lax.all_to_all(jnp.stack(fresh, 0), 'row', 0, 0)]
    all_to_all x2 -> x0, local copies, waits for them, and re-layouts: 15.8 us -> none  [per_device(): lax.all_to_all(grad_triple.reshape(col_rows, 3, 1, per_group), 'row', spl...]
  transfers between devices with their start and end apart: 16 -> 16, of which waited for: 9 -> 9; matrix products, arithmetic and copies ran while one was open for 27% -> 28% of each run, Pallas kernels for 0% -> 0%
where the time goes in v1:
time: 1160 us; the launch traced here: 1150 us
  matrix products  341 us (29%)
  waiting for transfers between devices  282 us (24%)
  blocking collectives  251 us (22%)
  other arithmetic  127 us (11%)
  local copies, waits for them, and re-layouts  108 us (9%)
  starting transfers between devices  20.7 us (2%)
  between operations  19 us (2%)
    unnamed x4, blocking collectives  132 us
    reduce_scatter x1, waiting for transfers between devices, per_device(): lax.psum_scatter(grad_fc2.astype(jnp.bfloat16), 'col', scatter_dimension=...  84.3 us
    convert_element_type x1, other arithmetic, clip_backward(): (weights_full * (grad_weights - row_delta)).astype(jnp.bfloat16)  64.7 us
    dot_general x1, matrix products, clip_backward(): jnp.einsum('qhd,khd->hqk', grad_mixed, value_rows, preferred_element_type...  56.5 us
    all_gather x1, blocking collectives, per_device(): lax.all_gather(w_fc2, 'row', axis=0, tiled=True)  55.4 us
    all_to_all x1, waiting for transfers between devices, lift_face(): moved = jax.lax.all_to_all(jnp.stack(fresh, 0), 'row', 0, 0)  48.5 us
    reduce_scatter x1, waiting for transfers between devices, per_device(): lax.psum_scatter(grad_qkv.astype(jnp.bfloat16), 'col', scatter_dimension=...  47.1 us
    dot_general x4, matrix products, inner_rows(): lax.dot_general(first, second, (((0,), (0,)), ((), ())), preferred_elemen...  46.3 us
  transfers between devices with their start and end apart: 16, of which 9 were waited for; matrix products, arithmetic and copies ran while one was open for 28% of the time, Pallas kernels for 0%

profile of v1, /device:TPU:0, one launch (start us, length us, event | category | flops | bytes accessed | tf_op | source)
XLA Modules:
  0.0 1149.1 jit_solution(12243304847570573564)
XLA Ops:
  7.2 10.6 all_gather.90
  17.9 5.2 all_gather.96
  23.2 8.9 all_gather.104
  41.7 5.4 all-reduce.37
  48.5 59.8 %all-reduce.35 = (bf16[1024]{0:T(1024)(128)(2,1)S(1)}, bf16[1024]{0:T(1024)(128)(2,1)S(1)}, bf16[1024]{0:T(1024)(128)(2,1)S(1)}, bf16[1024]{0:T(1024)(128)(2,1)S...) all-reduce(bf16[1024]{0:T(1024)(128)(2,1)S(1)} %dynamic-update-slic, ...), channel_id=1, replica_groups=mesh['row'=2,'col'=16] {'col'}, use_global_device_ids=true, to_apply=%add.7 | all-reduce | flops 7168 | bytes 28672
  110.8 10.2 add_convert_fusion
  121.0 12.0 %reshape.123 = bf16[784,3,2,512]{3,2,1,0:T(2,128)(2,1)} reshape(bf16[784,3072]{1,0:T(8,128)(2,1)} %add_convert_fusion) | data formatting | bytes 9633792 | tf_op jit(solution)/shard_map/reshape | solution.py:184
  132.9 5.4 copy.59
  138.3 6.0 all-to-all-start
  144.4 55.4 %all_gather.108 = bf16[4096,64]{0,1:T(8,128)(2,1)} all-gather(bf16[2048,64]{0,1:T(8,128)(2,1)S(1)} %copy-done.11), channel_id=1, replica_groups=mesh['row'=2,'col'=16] {'row'}, dimensions={0}, use_global_device_ids=true | all-gather | bytes 786432 | tf_op jit(solution)/shard_map/all_gather | solution.py:130
  199.8 14.3 %copy.60 = bf16[2,784,3,1,512]{1,0,4,2,3:T(2,128)(2,1)} copy(bf16[2,784,3,1,512]{4,1,2,0,3:T(8,128)(2,1)} %bitcast.3) | data formatting | bytes 9633792 | tf_op jit(solution)/shard_map/all_to_all | solution.py:185
  214.1 11.7 %squeeze.35 = bf16[1568,3,8,64]{0,3,2,1:T(8,128)(2,1)} reshape(bf16[2,784,3,1,512]{1,0,4,2,3:T(2,128)(2,1)} %copy.60) | data formatting | bytes 9633792 | tf_op jit(solution)/shard_map/while/body/jit(dynamic_index_in_dim)/squeeze | solution.py:189
  225.8 32.2 %multiply_reduce_fusion.1 = (f32[8,1568]{1,0:T(8,128)S(1)}, f32[8,1568,1568]{1,2,0:T(8,128)}) fusion(bf16[1568,3,8,64]{0,3,2,1:T(8,128)(2,1)} %squeeze.35), kind=kOutput, calls=%fused_computation.6 | convolution fusion | flops 2556956416 | bytes 82134016 | tf_op jit(solution)/shard_map/while/body/eval_jaxpr/qhd,khd->hqk/dot_general | solution.py:50
  258.0 26.7 %fusion = f32[8,1568]{1,0:T(8,128)S(1)} fusion(f32[8,1568,1568]{1,2,0:T(8,128)} %get-tuple-element.96, f32[8,1568]{1,0:T(8,128)S(1)} %get-tuple-element.95), kind=kLoop, calls=%fused_computation.5 | loop fusion | flops 58994432 | bytes 78776320 | tf_op jit(solution)/shard_map/while/body/eval_jaxpr/reduce_sum | solution.py:55
  284.8 30.6 %fusion.38 = bf16[8,64,1568]{2,1,0:T(8,128)(2,1)S(1)} fusion(f32[8,1568,1568]{1,2,0:T(8,128)} %get-tuple-element.96, f32[8,1568]{1,0:T(8,128)S(1)} %fusion, f32[8,1568]{1,0:T(8,128)S(1)} %get-tuple-element.95, bf16[1568,3,8,64]{0,3,2,1:T(8,128)(2,1)} %squeeze.35), kind=kOutput, calls=%fused_computation.71 | convolution fusion | flops 2597109760 | bytes 86902784 | tf_op jit(solution)/shard_map/while/body/eval_jaxpr/hqk,khd->qhd/dot_general | solution.py:57
  315.9 1.9 reduce.3
  319.3 2.1 reshape.232
  321.4 3.7 all-to-all-start.1
  325.1 14.4 %all-gather = bf16[2,1,128]{2,1,0:T(2,128)(2,1)S(1)} all-gather(bf16[1,1,128]{2,1,0:T(2,128)(2,1)S(1)} %bitcast.101), channel_id=1, replica_groups=mesh['row'=2,'col'=16] {'row'}, dimensions={0}, use_global_device_ids=true | all-gather | bytes 768 | tf_op jit(solution)/shard_map/all_gather | solution.py:138
  339.6 25.1 %all-gather.1 = bf16[16,1,256]{2,1,0:T(2,128)(2,1)S(1)} all-gather(bf16[1,1,256]{2,1,0:T(2,128)(2,1)S(1)} %bitcast.100), channel_id=1, replica_groups=mesh['row'=2,'col'=16] {'col'}, dimensions={0}, use_global_device_ids=true | all-gather | bytes 8704 | tf_op jit(solution)/shard_map/all_gather | solution.py:167
  364.7 2.5 reshape.233
  367.2 2.5 copy.76
  371.8 4.1 fusion.58
  378.2 39.0 %fusion.7 = (bf16[784,4096]{1,0:T(8,128)(2,1)}, f32[784,4096]{1,0:T(8,128)}) fusion(f32[4096]{0:T(1024)S(1)} %bitcast.98, bf16[1024,4096]{1,0:T(8,128)(2,1)} %all-gather.11.cloned.1.call-done, f32[784,1024]{1,0:T(8,128)} %copy-done.5, f32[1024]{0:T(1024)S(1)} %convert_element_type.194, f32[1024]{0:T(1024)S(1)} %convert_element_type.193, ...), kind=kOutput, calls=%fused_computation.14 | convolution fusion | flops 6792626176 | bytes 30898304 | tf_op jit(solution)/shard_map/dot_general | solution.py:201
  417.3 17.2 %fusion.59 = (bf16[4096]{0:T(1024)(128)(2,1)}, bf16[784,4096]{1,0:T(8,128)(2,1)}) fusion(f32[784,4096]{1,0:T(8,128)} %get-tuple-element.106, f32[4096]{0:T(1024)S(1)} %bitcast.99, bf16[4096,1024]{0,1:T(8,128)(2,1)} %all-gather.13.cloned.1.call-done, f32[784,1024]{1,0:T(8,128)S(1)} %copy-done.7), kind=kOutput, calls=%fused_computation.117 | convolution fusion | flops 6616002560 | bytes 30892032 | tf_op jit(solution)/shard_map/dot_general | solution.py:43
  434.5 11.0 multiply_reduce_fusion.2
  445.5 2.0 convert_reduce_fusion.1
  447.5 1.8 convolution_convert_fusion.4
  450.7 3.7 all-to-all-start.2
  454.4 20.3 %all-to-all-done.2 = bf16[784,2,512]{2,0,1:T(8,128)(2,1)S(1)} async-done(((bf16[784,2,512]{2,0,1:T(8,128)(2,1)}), bf16[784,2,512]{2,0,1:T(8,128)(2,1)S(1)}, u32[]{:S(2)}, u32[]{:S(2)}) %all-to-all-start.2) | async-done | bytes 1605664 | tf_op jit(solution)/shard_map/all_to_all | solution.py:236
  474.7 4.2 copy.65
  478.8 4.0 squeeze.39
  482.8 28.1 %fusion.41 = bf16[1568,1,8,64]{0,3,2,1:T(8,128)(2,1)S(1)} fusion(bf16[1568,8,64]{0,2,1:T(8,128)(2,1)S(1)} %squeeze.39, f32[8,1568,1568]{1,2,0:T(8,128)} %get-tuple-element.96, f32[8,1568]{1,0:T(8,128)S(1)} %log_add_fusion), kind=kOutput, calls=%fused_computation.76 | convolution fusion | flops 2577440768 | bytes 81937408 | tf_op jit(solution)/shard_map/while/body/eval_jaxpr/hqk,qhd->khd/dot_general | solution.py:71
  511.0 56.5 %multiply_reduce_fusion = (f32[8,1568]{1,0:T(8,128)S(1)}, f32[8,1568,1568]{1,2,0:T(8,128)}) fusion(f32[8,1568,1568]{1,2,0:T(8,128)} %get-tuple-element.96, f32[8,1568]{1,0:T(8,128)S(1)} %log_add_fusion, bf16[1568,8,64]{0,2,1:T(8,128)(2,1)S(1)} %squeeze.39, bf16[1568,3,8,64]{0,3,2,1:T(8,128)(2,1)} %squeeze.35), kind=kOutput, calls=%fused_computation.1 | convolution fusion | flops 2596294400 | bytes 165578752 | tf_op jit(solution)/shard_map/while/body/eval_jaxpr/qhd,khd->hqk/dot_general | solution.py:74
  567.5 64.7 %multiply_convert_fusion = bf16[8,1568,1568]{1,2,0:T(8,128)(2,1)} fusion(f32[8,1568,1568]{1,2,0:T(8,128)} %get-tuple-element.101, f32[8,1568,1568]{1,2,0:T(8,128)} %get-tuple-element.96, f32[8,1568]{1,0:T(8,128)S(1)} %get-tuple-element.100, f32[8,1568]{1,0:T(8,128)S(1)} %log_add_fusion), kind=kLoop, calls=%fused_computation | loop fusion | flops 98344960 | bytes 196790272 | tf_op jit(solution)/shard_map/while/body/eval_jaxpr/convert_element_type | solution.py:78
  632.3 19.4 %fusion.40 = bf16[1568,1,8,64]{0,3,2,1:T(8,128)(2,1)S(1)} fusion(bf16[8,1568,1568]{1,2,0:T(8,128)(2,1)} %multiply_convert_fusion, bf16[1568,3,8,64]{0,3,2,1:T(8,128)(2,1)} %squeeze.35), kind=kOutput, calls=%fused_computation.75 | convolution fusion | flops 2519236608 | bytes 45056000 | tf_op jit(solution)/shard_map/while/body/eval_jaxpr/hqk,qhd->khd/dot_general | solution.py:82
  651.7 21.0 %fusion.39 = bf16[1568,1,8,64]{0,3,2,1:T(8,128)(2,1)} fusion(bf16[8,1568,1568]{1,2,0:T(8,128)(2,1)} %multiply_convert_fusion, bf16[1568,3,8,64]{0,3,2,1:T(8,128)(2,1)} %squeeze.35), kind=kOutput, calls=%fused_computation.74 | convolution fusion | flops 2519236608 | bytes 45056000 | tf_op jit(solution)/shard_map/while/body/eval_jaxpr/hqk,khd->qhd/dot_general | solution.py:79
  672.7 2.2 pad_maximum_fusion
  674.9 3.3 fusion.55
  678.2 4.5 copy.69
  682.6 2.7 copy.70
  685.3 5.0 pad_maximum_fusion.1
  690.3 6.1 all-to-all-start.3
  696.5 5.1 convolution_convert_fusion.3
  701.9 48.5 %all-to-all-done.3 = bf16[2,784,3,1,512]{4,1,3,2,0:T(8,128)(2,1)} async-done(((bf16[2,784,3,1,512]{4,1,3,2,0:T(8,128)(2,1)}), bf16[2,784,3,1,512]{4,1,3,2,0:T(8,128)(2,1)}, u32[]{:S(2)}, u32[]{:S(2)}) %all-to-all-start.3) | async-done | bytes 4816928 | tf_op jit(solution)/shard_map/all_to_all | solution.py:109
  750.4 9.5 copy.71
  759.9 11.9 %reshape_reshape.3 = bf16[784,3072]{1,0:T(8,128)(2,1)} reshape(bf16[784,3,2,1,512]{4,2,1,0,3:T(2,128)(2,1)} %copy.71) | data formatting | bytes 9633792 | tf_op jit(solution)/shard_map/reshape;reshape | solution.py:245
  771.9 11.4 convolution_convert_fusion.2
  784.0 15.1 %convolution_convert_fusion.1 = bf16[1024,4096]{1,0:T(8,128)(2,1)} fusion(bf16[784,4096]{1,0:T(8,128)(2,1)} %get-tuple-element.104, f32[784,1024]{1,0:T(8,128)} %copy-done.5, f32[1024]{0:T(1024)S(1)} %copy-done.32, f32[1024]{0:T(1024)S(1)} %copy-done.23, f32[784]{0:T(1024)S(1)} %copy-done.25, f32[784]{0:T(1024)S(1)} %copy-done.17), kind=kOutput, calls=%fused_computation.38 | convolution fusion | flops 6584877056 | bytes 18036864 | tf_op jit(solution)/shard_map/dot_general | solution.py:37
  799.1 14.7 %convolution_convert_fusion = bf16[4096,1024]{0,1:T(8,128)(2,1)} fusion(bf16[784,4096]{1,0:T(8,128)(2,1)} %get-tuple-element.105, f32[784,1024]{1,0:T(8,128)} %param.29), kind=kOutput, calls=%fused_computation.37 | convolution fusion | flops 6581665792 | bytes 18022400 | tf_op jit(solution)/shard_map/dot_general | solution.py:37
  817.5 47.1 %reduce-scatter.9.cloned.1.call-done = bf16[1024,192]{0,1:T(8,128)(2,1)} async-done(((bf16[1024,3072]{0,1:T(8,128)(2,1)}), bf16[1024,192]{0,1:T(8,128)(2,1)}) %reduce-scatter.9.cloned.1.call-update) | async-done | bytes 393232 | tf_op jit(solution)/shard_map/reduce_scatter | solution.py:271
  864.9 10.5 fusion.33
  875.3 4.2 convert_element_type.218
  880.2 61.5 %all-reduce.34 = (bf16[1024]{0:T(1024)(128)(2,1)S(1)}, bf16[1024]{0:T(1024)(128)(2,1)S(1)}, bf16[1024]{0:T(1024)(128)(2,1)S(1)}, bf16[1024]{0:T(1024)(128)(2,1)S...) all-reduce(bf16[1024]{0:T(1024)(128)(2,1)S(1)} %dynamic-update-slic, ...), channel_id=1, replica_groups=mesh['row'=2,'col'=16] {'col'}, use_global_device_ids=true, to_apply=%add.15 | all-reduce | flops 13312 | bytes 53248
  941.7 30.1 %reduce-scatter.17.cloned.1.call-done = bf16[1024,256]{1,0:T(8,128)(2,1)} async-done(((bf16[1024,4096]{1,0:T(8,128)(2,1)}), bf16[1024,256]{1,0:T(8,128)(2,1)}) %reduce-scatter.17.cloned.1.call-update) | async-done | bytes 524304 | tf_op jit(solution)/shard_map/reduce_scatter | solution.py:277
  971.9 12.5 %add_convert_fusion.1 = bf16[784,1024]{1,0:T(8,128)(2,1)} fusion(f32[784,1024]{1,0:T(8,128)} %copy-done.5, f32[1024]{0:T(1024)S(1)} %convert_element_type.198, bf16[784,4096]{1,0:T(8,128)(2,1)} %get-tuple-element.105, bf16[4096,1024]{0,1:T(8,128)(2,1)} %all-gather.13.cloned.1.call-done), kind=kOutput, calls=%fused_computation.66 | convolution fusion | flops 6579077120 | bytes 19632128 | tf_op jit(solution)/shard_map/dot_general | solution.py:206
  985.1 5.0 all-reduce.36
  994.7 84.3 %reduce-scatter.21.cloned.1.call-done = bf16[4096,64]{0,1:T(8,128)(2,1)} async-done(((bf16[4096,1024]{0,1:T(8,128)(2,1)}), bf16[4096,64]{0,1:T(8,128)(2,1)}) %reduce-scatter.21.cloned.1.call-update) | async-done | bytes 524304 | tf_op jit(solution)/shard_map/reduce_scatter | solution.py:280
  1079.6 4.6 fusion.32
  1084.2 7.0 reduce-scatter.15.cloned.1.call-done
  1092.8 13.8 %reduce-scatter.11.cloned.1.call-done = bf16[512,192]{0,1:T(8,128)(2,1)} async-done(((bf16[1024,192]{0,1:T(8,128)(2,1)}), bf16[512,192]{0,1:T(8,128)(2,1)}) %reduce-scatter.11.cloned.1.call-update) | async-done | bytes 196624 | tf_op jit(solution)/shard_map/reduce_scatter | solution.py:326
  1108.3 15.2 %reduce-scatter.19.cloned.1.call-done = bf16[512,256]{1,0:T(8,128)(2,1)} async-done(((bf16[1024,256]{1,0:T(8,128)(2,1)}), bf16[512,256]{1,0:T(8,128)(2,1)}) %reduce-scatter.19.cloned.1.call-update) | async-done | bytes 262160 | tf_op jit(solution)/shard_map/reduce_scatter | solution.py:332
  1123.5 1.8 convert_element_type.211
  1125.3 15.0 %reduce-scatter.23.cloned.1.call-done = bf16[2048,64]{0,1:T(8,128)(2,1)} async-done(((bf16[4096,64]{0,1:T(8,128)(2,1)}), bf16[2048,64]{0,1:T(8,128)(2,1)}) %reduce-scatter.23.cloned.1.call-update) | async-done | bytes 262160 | tf_op jit(solution)/shard_map/reduce_scatter | solution.py:335
  (198 shorter events, 33.6 us)
Async XLA Ops:
  7.2 102.9 %copy-start = (bf16[784,1024]{1,0:T(8,128)(2,1)S(1)}, bf16[784,1024]{1,0:T(8,128)(2,1)}, u32[]{:S(2)}) copy-start(bf16[784,1024]{1,0:T(8,128)(2,1)} %param.15) | copy-start | bytes 4816900
  7.2 103.6 %all-gather.7.cloned.1.call-start = ((), (), s32[]{:S(2)}) async-start(), calls=%async_computation.12 | async-start | bytes 6684672 | tf_op jit(solution)/shard_map/all_gather | solution.py:156
  17.9 354.0 %all-gather.9.cloned.1.call-start = ((), (), s32[]{:S(2)}) async-start(), calls=%async_computation.13 | async-start | bytes 2228224 | tf_op jit(solution)/shard_map/all_gather | solution.py:157
  23.2 355.0 %all-gather.11.cloned.1.call-start = ((), (), s32[]{:S(2)}) async-start(), calls=%async_computation.14 | async-start | bytes 8912896 | tf_op jit(solution)/shard_map/all_gather | solution.py:158
  108.3 12.6 %copy-start.18 = (f32[1024]{0:T(1024)}, f32[1024]{0:T(1024)S(1)}, u32[]{:S(2)}) copy-start(f32[1024]{0:T(1024)S(1)} %convert_element_type.183) | copy-start | bytes 12292
  108.3 12.6 %copy-start.29 = (f32[1024]{0:T(1024)}, f32[1024]{0:T(1024)S(1)}, u32[]{:S(2)}) copy-start(f32[1024]{0:T(1024)S(1)} %convert_element_type.184) | copy-start | bytes 12292
  110.1 10.8 copy-start.14
  110.7 10.2 copy-start.20
  138.3 6.0 copy-start.11
  138.3 61.4 %all-to-all-start = ((bf16[784,3,2,512]{3,0,1,2:T(8,128)(2,1)}), bf16[784,3,2,512]{3,0,1,2:T(8,128)(2,1)}, u32[]{:S(2)}, u32[]{:S(2)}) async-start(bf16[784,3,2,512]{3,0,1,2:T(8,128)(2,1)} %copy.59), calls=%async_computation | async-start | bytes 9633792 | tf_op jit(solution)/shard_map/all_to_all | solution.py:185
  144.3 273.0 %all-gather.13.cloned.1.call-start = ((), (), s32[]{:S(2)}) async-start(), calls=%async_computation.15 | async-start | bytes 8912896 | tf_op jit(solution)/shard_map/all_gather | solution.py:159
  258.0 26.7 %copy-start.9 = (f32[8,1568]{1,0:T(8,128)}, f32[8,1568]{1,0:T(8,128)S(1)}, u32[]{:S(2)}) copy-start(f32[8,1568]{1,0:T(8,128)S(1)} %get-tuple-element.95) | copy-start | bytes 150532
  284.8 30.6 %copy-start.12 = (f32[8,1568]{1,0:T(8,128)}, f32[8,1568]{1,0:T(8,128)S(1)}, u32[]{:S(2)}) copy-start(f32[8,1568]{1,0:T(8,128)S(1)} %fusion) | copy-start | bytes 150532
  317.9 7.2 copy-start.35
  317.9 7.2 copy-start.34
  317.9 7.2 copy-start.33
  317.9 7.2 copy-start.40
  321.4 43.3 %all-to-all-start.1 = ((bf16[2,2,200704]{2,1,0:T(2,128)(2,1)}), bf16[2,2,200704]{2,1,0:T(2,128)(2,1)S(1)}, u32[]{:S(2)}, u32[]{:S(2)}) async-start(bf16[2,2,200704]{2,1,0:T(2,128)(2,1)} %reshape.232), calls=%async_computation.1 | async-start | bytes 3211264 | tf_op jit(solution)/shard_map/all_to_all | solution.py:190
  325.1 120.4 %copy-start.22 = (f32[1024]{0:T(1024)}, f32[1024]{0:T(1024)S(1)}, u32[]{:S(2)}) copy-start(f32[1024]{0:T(1024)S(1)} %convert_element_type.193) | copy-start | bytes 12292
  325.1 53.1 %copy-start.31 = (f32[1024]{0:T(1024)}, f32[1024]{0:T(1024)S(1)}, u32[]{:S(2)}) copy-start(f32[1024]{0:T(1024)S(1)} %convert_element_type.194) | copy-start | bytes 12292
  367.2 4.6 copy-start.1
  371.8 4.2 copy-start.8
  376.0 1.7 copy-start.5
  376.0 69.5 %copy-start.16 = (f32[784]{0:T(1024)}, f32[784]{0:T(1024)S(1)}, u32[]{:S(2)}) copy-start(f32[784]{0:T(1024)S(1)} %broadcast_multiply_fusion.4) | copy-start | bytes 9412
  378.2 67.3 %copy-start.24 = (f32[784]{0:T(1024)}, f32[784]{0:T(1024)S(1)}, u32[]{:S(2)}) copy-start(f32[784]{0:T(1024)S(1)} %add_rsqrt_fusion) | copy-start | bytes 9412
  378.2 39.0 %copy-start.7 = (f32[784,1024]{1,0:T(8,128)S(1)}, f32[784,1024]{1,0:T(8,128)}, u32[]{:S(2)}) copy-start(f32[784,1024]{1,0:T(8,128)} %param.29) | copy-start | bytes 9633796
  417.3 17.2 %copy-start.6 = (f32[784,1024]{1,0:T(8,128)S(1)}, f32[784,1024]{1,0:T(8,128)}, u32[]{:S(2)}) copy-start(f32[784,1024]{1,0:T(8,128)} %copy-done.5) | copy-start | bytes 9633796
  417.3 17.2 %copy-start.38 = (bf16[1024,4096]{1,0:T(8,128)(2,1)S(1)}, bf16[1024,4096]{1,0:T(8,128)(2,1)}, u32[]{:S(2)}) copy-start(bf16[1024,4096]{1,0:T(8,128)(2,1)} %all-gather.11.cloned.1.call-done) | copy-start | bytes 25165828
  445.5 2.0 copy-start.39
  447.5 1.8 copy-start.3
  449.4 5.0 copy-start.10
  449.4 5.0 copy-start.13
  450.7 24.0 %all-to-all-start.2 = ((bf16[784,2,512]{2,0,1:T(8,128)(2,1)}), bf16[784,2,512]{2,0,1:T(8,128)(2,1)S(1)}, u32[]{:S(2)}, u32[]{:S(2)}) async-start(bf16[784,2,512]{2,0,1:T(8,128)(2,1)} %bitcast.88), calls=%async_computation.2 | async-start | bytes 3211264 | tf_op jit(solution)/shard_map/all_to_all | solution.py:236
  690.3 6.1 copy-start.4
  690.3 60.1 %all-to-all-start.3 = ((bf16[2,784,3,1,512]{4,1,3,2,0:T(8,128)(2,1)}), bf16[2,784,3,1,512]{4,1,3,2,0:T(8,128)(2,1)}, u32[]{:S(2)}, u32[]{:S(2)}) async-start(bf16[2,784,3,1,512]{4,1,3,2,0:T(8,128)(2,1)} %pad_maximum_fusion.1), calls=%async_computation.3 | async-start | bytes 9633792 | tf_op jit(solution)/shard_map/all_to_all | solution.py:109
  696.4 117.5 %reduce-scatter.13.cloned.1.call-start = ((), (), s32[]{:S(2)}) async-start(), calls=%async_computation.18 | async-start | bytes 2228224 | tf_op jit(solution)/shard_map/reduce_scatter | solution.py:274
  701.6 163.0 %reduce-scatter.9.cloned.1.call-start = ((), (), s32[]{:S(2)}) async-start(), calls=%async_computation.16 | async-start | bytes 6684672 | tf_op jit(solution)/shard_map/reduce_scatter | solution.py:271
  759.9 12.0 %copy-start.2 = (bf16[784,1024]{1,0:T(8,128)(2,1)S(1)}, bf16[784,1024]{1,0:T(8,128)(2,1)}, u32[]{:S(2)}) copy-start(bf16[784,1024]{1,0:T(8,128)(2,1)} %param.15) | copy-start | bytes 4816900
  759.9 12.0 %copy-start.15 = (f32[784]{0:T(1024)S(1)}, f32[784]{0:T(1024)}, u32[]{:S(2)}) copy-start(f32[784]{0:T(1024)} %copy-done.14) | copy-start | bytes 9412
  759.9 12.0 %copy-start.19 = (f32[1024]{0:T(1024)S(1)}, f32[1024]{0:T(1024)}, u32[]{:S(2)}) copy-start(f32[1024]{0:T(1024)} %copy-done.18) | copy-start | bytes 12292
  759.9 12.0 %copy-start.21 = (f32[784]{0:T(1024)S(1)}, f32[784]{0:T(1024)}, u32[]{:S(2)}) copy-start(f32[784]{0:T(1024)} %copy-done.20) | copy-start | bytes 9412
  759.9 12.0 %copy-start.30 = (f32[1024]{0:T(1024)S(1)}, f32[1024]{0:T(1024)}, u32[]{:S(2)}) copy-start(f32[1024]{0:T(1024)} %copy-done.29) | copy-start | bytes 12292
  783.3 0.7 copy-start.17
  783.3 0.7 copy-start.23
  783.3 0.7 copy-start.25
  783.3 0.7 copy-start.32
  783.3 188.5 %reduce-scatter.17.cloned.1.call-start = ((), (), s32[]{:S(2)}) async-start(), calls=%async_computation.20 | async-start | bytes 8912896 | tf_op jit(solution)/shard_map/reduce_scatter | solution.py:277
  799.1 279.9 %reduce-scatter.21.cloned.1.call-start = ((), (), s32[]{:S(2)}) async-start(), calls=%async_computation.22 | async-start | bytes 8912896 | tf_op jit(solution)/shard_map/reduce_scatter | solution.py:280
  813.8 3.4 copy-start.41
  813.9 277.4 %reduce-scatter.15.cloned.1.call-start = ((), (), s32[]{:S(2)}) async-start(), calls=%async_computation.19 | async-start | bytes 196608 | tf_op jit(solution)/shard_map/reduce_scatter | solution.py:329
  814.6 292.0 %reduce-scatter.11.cloned.1.call-start = ((), (), s32[]{:S(2)}) async-start(), calls=%async_computation.17 | async-start | bytes 589824 | tf_op jit(solution)/shard_map/reduce_scatter | solution.py:326
  864.6 258.9 %reduce-scatter.19.cloned.1.call-start = ((), (), s32[]{:S(2)}) async-start(), calls=%async_computation.21 | async-start | bytes 786432 | tf_op jit(solution)/shard_map/reduce_scatter | solution.py:332
  879.5 0.7 copy-start.26
  879.5 0.7 copy-start.27
  879.5 0.7 copy-start.28
  879.5 0.7 copy-start.36
  879.5 0.7 copy-start.37
  971.9 168.4 %reduce-scatter.23.cloned.1.call-start = ((), (), s32[]{:S(2)}) async-start(), calls=%async_computation.23 | async-start | bytes 786432 | tf_op jit(solution)/shard_map/reduce_scatter | solution.py:335
Sparse Core Ops, SparseCore 0:
  18.0 62.1 all-gather.6
  82.3 40.4 all-gather.8
  125.0 76.9 all-gather.10
  204.0 72.4 all-gather.12
  701.7 59.4 reduce-scatter.12
  783.4 81.1 reduce-scatter.8
  868.7 103.1 reduce-scatter.16
  975.9 103.0 reduce-scatter.20
  1081.2 9.9 reduce-scatter.14
  1093.3 13.1 reduce-scatter.10
  1108.8 14.6 reduce-scatter.18
  1125.6 14.6 reduce-scatter.22
